TPU v7x, 256 devices: a whole 4x4x8 slice. The times are simulated.
256 devices in a mesh: dp: 8 (over z_lo, y), seq: 32 (over x, z_hi, core).
Axes of the slice: x: 4, y: 4, z: 8 (z_hi: 4, z_lo: 2; z = z_hi * 2 + z_lo), core: 2. Of those that a mesh axis runs over, the one named last changes fastest.
Arguments:
- tokens: bfloat16 [8, 8192, 4096], P('dp', 'seq'), may hold values from -6 to 6
- queries: bfloat16 [8, 8192, 128], P('dp', 'seq'), may hold values from -6 to 6
- key_vectors: bfloat16 [8, 8192, 128], P('dp', 'seq'), may hold values from -6 to 6
- doc_position: int32 [8, 8192], P('dp', 'seq'), may hold values from 0 to 8191, as said below
- value_scores: float32 [8, 8192, 4], P('dp', 'seq'), may hold values from 0.1 to 1
- value_experts: int32 [8, 8192, 2], P('dp', 'seq'), may hold values from 0 to 3, all different within a row
- output_scores: float32 [8, 8192, 4], P('dp', 'seq'), may hold values from 0.1 to 1
- output_experts: int32 [8, 8192, 2], P('dp', 'seq'), may hold values from 0 to 3, all different within a row
- value_panels: bfloat16 [4096, 512], P('seq'), may hold values from -0.09375 to 0.09375
- output_panels: bfloat16 [4096, 512], P('seq'), may hold values from -3 to 3
- cotangent: bfloat16 [8, 8192, 4096], P('dp', 'seq'), may hold values from -0.625 to 0.625
Outputs:
- layer_output: bfloat16 [8, 8192, 4096], P('dp', 'seq')
- grad_tokens: bfloat16 [8, 8192, 4096], P('dp', 'seq')
- grad_queries: bfloat16 [8, 8192, 128], P('dp', 'seq')
- grad_keys: bfloat16 [8, 8192, 128], P('dp', 'seq')
- grad_value: float32 [4096, 512], P('seq')
- grad_output: float32 [4096, 512], P('seq')
Inputs may be any that keep to these rules, and one draw needn't show every extreme that they name: doc_position[b, i] is i minus the first position of the document that holds position i; position 0 starts a document in every sequence; sequence 0 is one document; every other sequence holds one to four documents.
All inputs are finite; a program needn't handle non-finite values.
Results may differ from a plain program's by a relative error of at most 0.035.
Values may be sent and summed in bfloat16 or wider, within the bound.
No kernel may reach another device: no remote copies, remote signals or barrier semaphores. Data moves between devices by JAX's collectives and lax.ppermute only.
A program may use at most 128 MiB of HBM per device.

v0:
```python
import jax
import jax.numpy as jnp
from jax import lax
from jax.sharding import PartitionSpec as P


def expert_gates(scores, chosen, experts):
    chosen_hit = chosen[:, :, None] == lax.iota(jnp.int32, experts)[None, None, :]
    return jnp.where(jnp.any(chosen_hit, axis=1), scores, jnp.float32(0.0))


def contract_last(left, right):
    return lax.dot_general(
        left, right, (((1,), (1,)), ((), ())), preferred_element_type=jnp.float32
    )


def contract_first(left, right):
    return lax.dot_general(
        left, right, (((0,), (0,)), ((), ())), preferred_element_type=jnp.float32
    )


def body(
    tokens,
    queries,
    key_vectors,
    doc_position,
    value_scores,
    value_experts,
    output_scores,
    output_experts,
    value_panels,
    output_panels,
    cotangent,
):
    tok_block = tokens[0]
    query_block = queries[0]
    own_keys = key_vectors[0]
    positions = doc_position[0]
    grad_rows = cotangent[0]
    tok_rows = tok_block.shape[0]
    head_size = query_block.shape[1]
    experts = value_scores.shape[2]
    panel_width = value_panels.shape[1]
    value_gate = expert_gates(value_scores[0], value_experts[0], experts)
    output_gate = expert_gates(output_scores[0], output_experts[0], experts)
    value_full, output_full = (
        lax.all_gather(value_panels, "seq", axis=0, tiled=True),
        lax.all_gather(output_panels, "seq", axis=0, tiled=True),
    )
    projection = jnp.dot(tok_block, value_full, preferred_element_type=jnp.float32)
    value_vec = jnp.sum(
        projection.reshape(tok_rows, experts, head_size) * value_gate[:, :, None], axis=1
    ).astype(jnp.bfloat16)
    keys_all, values_all = (
        lax.all_gather(own_keys, "seq", axis=0, tiled=True),
        lax.all_gather(value_vec, "seq", axis=0, tiled=True),
    )
    length = keys_all.shape[0]
    score_scale = head_size ** (-0.5)
    query_index = lax.axis_index("seq") * tok_rows + lax.iota(jnp.int32, tok_rows)
    key_index = lax.iota(jnp.int32, length)
    visible = (key_index[None, :] <= query_index[:, None]) & (
        query_index[:, None] - key_index[None, :] <= positions[:, None]
    )
    masked = jnp.where(visible, contract_last(query_block, keys_all) * score_scale, -jnp.inf)
    row_max = jnp.max(masked, axis=1)
    log_total = row_max + jnp.log(jnp.sum(jnp.exp(masked - row_max[:, None]), axis=1))
    attn_prob = jnp.exp(masked - log_total[:, None])
    prob_low = attn_prob.astype(jnp.bfloat16)
    attended = jnp.dot(prob_low, values_all, preferred_element_type=jnp.float32).astype(
        jnp.bfloat16
    )
    expanded = (
        (output_gate[:, :, None] * attended.astype(jnp.float32)[:, None, :])
        .reshape(tok_rows, panel_width)
        .astype(jnp.bfloat16)
    )
    layer_output = contract_last(expanded, output_full).astype(jnp.bfloat16)
    pulled = jnp.dot(grad_rows, output_full, preferred_element_type=jnp.float32)
    dattended = jnp.sum(
        pulled.reshape(tok_rows, experts, head_size) * output_gate[:, :, None], axis=1
    ).astype(jnp.bfloat16)
    row_delta = jnp.sum(dattended.astype(jnp.float32) * attended.astype(jnp.float32), axis=1)
    dweights = contract_last(dattended, values_all)
    dscores = (attn_prob * (dweights - row_delta[:, None])).astype(jnp.bfloat16)
    grad_queries = (
        jnp.dot(dscores, keys_all, preferred_element_type=jnp.float32) * score_scale
    ).astype(jnp.bfloat16)
    key_term = contract_first(dscores, query_block) * score_scale
    value_term = contract_first(prob_low, dattended)
    dkey_sum, dvalue_sum = (
        lax.psum_scatter(
            key_term.astype(jnp.bfloat16), "seq", scatter_dimension=0, tiled=True
        ).astype(jnp.float32),
        lax.psum_scatter(
            value_term.astype(jnp.bfloat16), "seq", scatter_dimension=0, tiled=True
        ).astype(jnp.float32),
    )
    grad_keys = dkey_sum.astype(jnp.bfloat16)
    dvalue = dvalue_sum.astype(jnp.bfloat16)
    value_grad = (
        (value_gate[:, :, None] * dvalue.astype(jnp.float32)[:, None, :])
        .reshape(tok_rows, panel_width)
        .astype(jnp.bfloat16)
    )
    grad_tokens = contract_last(value_grad, value_full).astype(jnp.bfloat16)
    term_value = contract_first(tok_block, value_grad)
    term_output = contract_first(grad_rows, expanded)
    owned = lax.psum_scatter(
        jnp.concatenate([term_value, term_output], axis=1).astype(jnp.bfloat16),
        "seq",
        scatter_dimension=0,
        tiled=True,
    )
    summed = lax.psum(owned, "dp").astype(jnp.float32)
    return (
        layer_output[None],
        grad_tokens[None],
        grad_queries[None],
        grad_keys[None],
        summed[:, :panel_width],
        summed[:, panel_width:],
    )


def solution(mesh):
    in_specs = (
        P("dp", "seq", None),
        P("dp", "seq", None),
        P("dp", "seq", None),
        P("dp", "seq"),
        P("dp", "seq", None),
        P("dp", "seq", None),
        P("dp", "seq", None),
        P("dp", "seq", None),
        P("seq", None),
        P("seq", None),
        P("dp", "seq", None),
    )
    out_specs = (
        P("dp", "seq", None),
        P("dp", "seq", None),
        P("dp", "seq", None),
        P("dp", "seq", None),
        P("seq", None),
        P("seq", None),
    )
    return jax.shard_map(body, mesh=mesh, in_specs=in_specs, out_specs=out_specs, check_vma=False)
```

profile of v0, /device:TPU:1, one launch (start us, length us, event | category | flops | bytes accessed | tf_op | source)
XLA Modules:
  0.0 666.1 jit_solution(10940611194924719588)
XLA Ops:
  10.9 58.7 %all-gather.12.cloned.1.call-done = bf16[1,8192,128]{2,1,0:T(8,128)(2,1)} async-done(((bf16[1,256,128]{2,1,0:T(8,128)(2,1)}), bf16[1,8192,128]{2,1,0:T(8,128)(2,1)}) %all-gather.12.cloned.1.call-update) | async-done | bytes 2097168 | tf_op jit(solution)/shard_map/all_gather | solution.py:57
  69.5 4.6 fusion.50
  75.5 1.9 copy-done.2
  77.4 52.2 %all-gather.10.cloned.1.call-done = bf16[4096,512]{1,0:T(8,128)(2,1)} async-done(((bf16[128,512]{1,0:T(8,128)(2,1)}), bf16[4096,512]{1,0:T(8,128)(2,1)}) %all-gather.10.cloned.1.call-update) | async-done | bytes 4194320 | tf_op jit(solution)/shard_map/all_gather | solution.py:50
  129.5 6.4 copy.46
  135.9 4.1 fusion.25
  140.2 6.6 convolution_convert_fusion
  147.0 43.1 %all-gather.6.cloned.1.call-done = bf16[4096,512]{1,0:T(8,128)(2,1)} async-done(((bf16[128,512]{1,0:T(8,128)(2,1)}), bf16[4096,512]{1,0:T(8,128)(2,1)}) %all-gather.6.cloned.1.call-update) | async-done | bytes 4194320 | tf_op jit(solution)/shard_map/all_gather | solution.py:49
  190.0 6.4 copy.43
  196.4 4.1 fusion.28
  200.8 80.0 %reduce-scatter.6.cloned.1.call-done = bf16[256,128]{1,0:T(8,128)(2,1)} async-done(((bf16[8192,128]{1,0:T(8,128)(2,1)}), bf16[256,128]{1,0:T(8,128)(2,1)}) %reduce-scatter.6.cloned.1.call-update) | async-done | bytes 65552 | tf_op jit(solution)/shard_map/reduce_scatter | solution.py:97
  282.0 3.2 fusion.6
  285.2 53.2 %all-gather.8.cloned.1.call-done = bf16[8192,128]{1,0:T(8,128)(2,1)} async-done(((bf16[256,128]{1,0:T(8,128)(2,1)}), bf16[8192,128]{1,0:T(8,128)(2,1)}) %all-gather.8.cloned.1.call-update) | async-done | bytes 2097168 | tf_op jit(solution)/shard_map/all_gather | solution.py:58
  338.5 5.7 multiply_reduce_fusion
  344.7 3.2 fusion.7
  347.9 7.8 %pad_maximum_fusion = bf16[4096,1024]{0,1:T(8,128)(2,1)} fusion(bf16[4096,512]{0,1:T(8,128)(2,1)} %fusion.7, bf16[4096,512]{0,1:T(8,128)(2,1)} %fusion.6), kind=kLoop, calls=%fused_computation.8 | loop fusion | flops 16777216 | bytes 16777216 | tf_op jit(solution)/shard_map/concatenate | solution.py:112
  355.7 12.0 %copy.51 = bf16[4096,1024]{1,0:T(8,128)(2,1)} copy(bf16[4096,1024]{0,1:T(8,128)(2,1)} %pad_maximum_fusion) | data formatting | bytes 16777216
  369.3 6.1 fusion.2
  375.3 109.9 %reduce-scatter.10.cloned.1.call-done = bf16[128,1024]{1,0:T(8,128)(2,1)} async-done(((bf16[4096,1024]{1,0:T(8,128)(2,1)}), bf16[128,1024]{1,0:T(8,128)(2,1)}) %reduce-scatter.10.cloned.1.call-update) | async-done | bytes 262160
  487.3 4.8 fusion.3
  492.1 5.0 fusion.9
  497.1 2.6 fusion.8
  502.6 58.4 %all-reduce.2.cloned.1.call-done = bf16[128,1024]{0,1:T(8,128)(2,1)} async-done(((bf16[128,1024]{0,1:T(8,128)(2,1)}), bf16[128,1024]{0,1:T(8,128)(2,1)}) %all-reduce.2.cloned.1.call-update) | async-done | bytes 262160 | tf_op jit(solution)/shard_map/psum | solution.py:117
  563.7 95.6 %reduce-scatter.8.cloned.1.call-done = bf16[256,128]{1,0:T(8,128)(2,1)} async-done(((bf16[8192,128]{1,0:T(8,128)(2,1)}), bf16[256,128]{1,0:T(8,128)(2,1)}) %reduce-scatter.8.cloned.1.call-update) | async-done | bytes 65552 | tf_op jit(solution)/shard_map/reduce_scatter | solution.py:94
  (56 shorter events, 16.3 us)
Async XLA Ops:
  7.2 189.3 %copy-start = (bf16[1,256,4096]{2,1,0:T(8,128)(2,1)S(1)}, bf16[1,256,4096]{2,1,0:T(8,128)(2,1)}, u32[]{:S(2)}) copy-start(bf16[1,256,4096]{2,1,0:T(8,128)(2,1)} %param.11) | copy-start | bytes 6291460
  7.2 62.3 %all-gather.12.cloned.1.call-start = ((), (), s32[]{:S(2)}) async-start(), calls=%async_computation.9 | async-start | bytes 2162688 | tf_op jit(solution)/shard_map/all_gather | solution.py:57
  7.9 121.6 %all-gather.10.cloned.1.call-start = ((), (), s32[]{:S(2)}) async-start(), calls=%async_computation.5 | async-start | bytes 4325376 | tf_op jit(solution)/shard_map/all_gather | solution.py:50
  8.7 181.4 %all-gather.6.cloned.1.call-start = ((), (), s32[]{:S(2)}) async-start(), calls=%async_computation.3 | async-start | bytes 4325376 | tf_op jit(solution)/shard_map/all_gather | solution.py:49
  9.4 271.4 %reduce-scatter.6.cloned.1.call-start = ((), (), s32[]{:S(2)}) async-start(), calls=%async_computation.6 | async-start | bytes 2162688 | tf_op jit(solution)/shard_map/reduce_scatter | solution.py:97
  74.1 3.2 copy-start.2
  140.2 6.8 %copy-start.10 = (s32[1,256,2]{1,2,0:T(2,128)S(1)}, s32[1,256,2]{1,2,0:T(2,128)}, u32[]{:S(2)}) copy-start(s32[1,256,2]{1,2,0:T(2,128)} %param.16) | copy-start | bytes 6148
  140.2 6.8 %copy-start.9 = (f32[1,256,4]{1,2,0:T(4,128)S(1)}, f32[1,256,4]{1,2,0:T(4,128)}, u32[]{:S(2)}) copy-start(f32[1,256,4]{1,2,0:T(4,128)} %param.15) | copy-start | bytes 12292
  146.9 191.6 %all-gather.8.cloned.1.call-start = ((), (), s32[]{:S(2)}) async-start(), calls=%async_computation.4 | async-start | bytes 2162688 | tf_op jit(solution)/shard_map/all_gather | solution.py:58
  200.6 284.6 %reduce-scatter.10.cloned.1.call-start = ((), (), s32[]{:S(2)}) async-start(), calls=%async_computation.10 | async-start | bytes 8650752
  285.2 59.4 %copy-start.6 = (bf16[1,256,4096]{2,1,0:T(8,128)(2,1)S(1)}, bf16[1,256,4096]{2,1,0:T(8,128)(2,1)}, u32[]{:S(2)}) copy-start(bf16[1,256,4096]{2,1,0:T(8,128)(2,1)} %param.21) | copy-start | bytes 6291460
  367.7 1.6 copy-start.5
  367.7 193.3 %all-reduce.2.cloned.1.call-start = ((), (), s32[]{:S(2)}) async-start(), calls=%async_computation.8 | async-start | bytes 524288 | tf_op jit(solution)/shard_map/psum | solution.py:117
  369.3 118.0 %copy-start.8 = (bf16[1,256,128]{2,1,0:T(8,128)(2,1)S(1)}, bf16[1,256,128]{2,1,0:T(8,128)(2,1)}, u32[]{:S(2)}) copy-start(bf16[1,256,128]{2,1,0:T(8,128)(2,1)} %param.12) | copy-start | bytes 196612
  487.0 172.3 %reduce-scatter.8.cloned.1.call-start = ((), (), s32[]{:S(2)}) async-start(), calls=%async_computation.7 | async-start | bytes 2162688 | tf_op jit(solution)/shard_map/reduce_scatter | solution.py:94
  492.1 5.0 copy-start.4
  497.1 2.6 copy-start.3
  497.1 3.7 copy-start.7
  497.1 162.2 %copy-start.1 = (bf16[1,256,4096]{2,1,0:T(8,128)(2,1)S(1)}, bf16[1,256,4096]{2,1,0:T(8,128)(2,1)}, u32[]{:S(2)}) copy-start(bf16[1,256,4096]{2,1,0:T(8,128)(2,1)} %param.11) | copy-start | bytes 6291460
Sparse Core Ops, SparseCore 0:
  10.6 58.8 all-gather.11
  72.1 57.4 all-gather.9
  132.1 57.8 all-gather.5
  194.3 86.4 reduce-scatter.5
  283.8 54.6 all-gather.7
  367.8 117.3 reduce-scatter.9
  488.5 72.4 all-reduce.1
  565.4 93.8 reduce-scatter.7
where the time goes:
time: 668 us; the launch traced here: 666 us
  waiting for transfers between devices  553 us (83%)
  matrix products  52 us (8%)
  local copies, waits for them, and re-layouts  34.2 us (5%)
  between operations  14.3 us (2%)
  other arithmetic  11.8 us (2%)
    unnamed x9, waiting for transfers between devices  112 us
    reduce_scatter x1, waiting for transfers between devices, body(): lax.psum_scatter(key_term.astype(jnp.bfloat16), 'seq', scatter_dimension=...  95.6 us
    reduce_scatter x1, waiting for transfers between devices, body(): lax.psum_scatter(value_term.astype(jnp.bfloat16), 'seq', scatter_dimensio...  80 us
    all_gather x1, waiting for transfers between devices, body(): lax.all_gather(own_keys, 'seq', axis=0, tiled=True)  58.7 us
    psum x1, waiting for transfers between devices, body(): summed = lax.psum(owned, 'dp').astype(jnp.float32)  58.4 us
    all_gather x1, waiting for transfers between devices, body(): lax.all_gather(value_vec, 'seq', axis=0, tiled=True)  53.2 us
    all_gather x1, waiting for transfers between devices, body(): lax.all_gather(output_panels, 'seq', axis=0, tiled=True)  52.2 us
    all_gather x1, waiting for transfers between devices, body(): lax.all_gather(value_panels, 'seq', axis=0, tiled=True)  43.1 us
  transfers between devices with their start and end apart: 8, of which 8 were waited for; matrix products, arithmetic and copies ran while one was open for 9% of the time, Pallas kernels for 0%

commit v1 on v0

v1 whole, which is shorter than its diff:
```python
import jax
import jax.numpy as jnp
from jax import lax
from jax.sharding import Mesh, PartitionSpec as P

F32 = jnp.float32
BF16 = jnp.bfloat16


def expert_gates(scores, chosen, experts):
    chosen_hit = chosen[:, :, None] == lax.iota(jnp.int32, experts)[None, None, :]
    return jnp.where(jnp.any(chosen_hit, axis=1), scores, F32(0.0))


def contract_last(left, right):
    return lax.dot_general(left, right, (((1,), (1,)), ((), ())), preferred_element_type=F32)


def contract_first(left, right):
    return lax.dot_general(left, right, (((0,), (0,)), ((), ())), preferred_element_type=F32)


def exchange(blocks, axes):
    return lax.all_to_all(blocks, axes, 0, 0, tiled=True)


def share(block, axes, count):
    return exchange(jnp.broadcast_to(block[None], (count,) + block.shape), axes)


def other_core(value):
    return lax.ppermute(value, "c", [(0, 1), (1, 0)])


def body(
    tokens,
    queries,
    key_vectors,
    doc_position,
    value_scores,
    value_experts,
    output_scores,
    output_experts,
    value_panels,
    output_panels,
    cotangent,
):
    n_x, n_y, n_zh, n_zl = 4, 4, 4, 2
    tok_block = tokens[0]
    query_block = queries[0]
    own_keys = key_vectors[0]
    positions = doc_position[0]
    grad_rows = cotangent[0]
    rows, width = tok_block.shape
    head = query_block.shape[1]
    experts = value_scores.shape[2]
    panel_rows, panel_width = value_panels.shape
    half = panel_width // 2
    ix, izh, ic = lax.axis_index("x"), lax.axis_index("zh"), lax.axis_index("c")
    first = ic == 0

    def own_first(pair):
        return jnp.where(first, pair, pair[::-1])

    def gate_own_first(gate):
        return own_first(gate.T.reshape(2, experts // 2, rows)).reshape(experts, rows).T

    value_gate = gate_own_first(expert_gates(value_scores[0], value_experts[0], experts))
    output_gate = expert_gates(output_scores[0], output_experts[0], experts)
    output_gate_own = gate_own_first(output_gate)

    output_full = lax.all_gather(output_panels, ("x", "zh", "c"), axis=0, tiled=True)

    mine = lax.dynamic_slice_in_dim(value_panels, ic * half, half, 1)
    theirs = lax.dynamic_slice_in_dim(value_panels, (1 - ic) * half, half, 1)
    half_rows = own_first(jnp.stack([mine, other_core(theirs)])).reshape(2 * panel_rows, half)
    pos_hi = (positions // 128).astype(BF16)
    pos_lo = (positions % 128).astype(BF16)
    pos_rows = jnp.zeros((16, half + head), BF16)
    pos_rows = pos_rows.at[0, :rows].set(pos_hi).at[1, :rows].set(pos_lo)
    packed = jnp.concatenate(
        [jnp.concatenate([half_rows, query_block], axis=1), pos_rows], axis=0
    )
    packed = share(packed, "zh", n_zh)
    panels_zh = packed[:, :rows, :half].reshape(n_zh * rows, half)
    queries_zh = packed[:, :rows, half:].reshape(n_zh * rows, head)
    pos_zh = packed[:, rows : rows + 2, :rows]
    key_rows = jnp.concatenate([own_keys[: rows // 2], own_keys[rows // 2 :]], axis=1)
    packed = share(jnp.concatenate([panels_zh, key_rows], axis=0), "x", n_x)
    value_mine = packed[:, : n_zh * rows].reshape(width, half)
    key_got = packed[:, n_zh * rows :]
    keys_x = jnp.concatenate([key_got[:, :, :head], key_got[:, :, head:]], axis=1).reshape(
        n_x * rows, head
    )
    value_own = jnp.concatenate([value_mine, other_core(value_mine)], axis=1)
    queries_all = jnp.concatenate([queries_zh, other_core(queries_zh)], axis=0)
    pos_pair = jnp.stack([pos_zh, other_core(pos_zh)]).astype(F32)
    pos_all = (pos_pair[:, :, 0] * 128.0 + pos_pair[:, :, 1]).astype(jnp.int32).reshape(-1)

    count = queries_all.shape[0]
    scale = head ** (-0.5)
    core_of = own_first(jnp.arange(2, dtype=jnp.int32))
    query_index = (
        ((ix * n_zh + jnp.arange(n_zh, dtype=jnp.int32))[None, :, None] * 2 + core_of[:, None, None])
        * rows
        + jnp.arange(rows, dtype=jnp.int32)[None, None, :]
    ).reshape(-1)
    key_index = (
        ((jnp.arange(n_x, dtype=jnp.int32) * n_zh + izh) * 2 + ic)[:, None] * rows
        + jnp.arange(rows, dtype=jnp.int32)[None, :]
    ).reshape(-1)
    visible = (key_index[:, None] <= query_index[None, :]) & (
        key_index[:, None] >= (query_index - pos_all)[None, :]
    )
    masked = jnp.where(visible, contract_last(keys_x, queries_all) * scale, -jnp.inf)
    top = jnp.maximum(jnp.max(masked, axis=0), -1e30)
    total = jnp.sum(jnp.exp(masked - top[None, :]), axis=0)
    stats = jnp.stack([top, total]).reshape(2, 2, count // 2)
    stats = jnp.where(first, stats, stats[:, ::-1])
    stats = share(stats, ("zh", "c"), n_zh * 2)
    all_top = jnp.max(stats[:, 0], axis=0)
    all_total = jnp.sum(stats[:, 1] * jnp.exp(stats[:, 0] - all_top[None]), axis=0)
    log_total = own_first(all_top + jnp.log(all_total)).reshape(-1)
    attn_prob = jnp.exp(masked - log_total[None, :])
    prob_low = attn_prob.astype(BF16)

    projection = jnp.dot(tok_block, value_own, preferred_element_type=F32)
    value_vec = jnp.sum(
        projection.reshape(rows, experts, head) * value_gate[:, :, None], axis=1
    ).astype(BF16)
    values_x = share(value_vec, "x", n_x).reshape(n_x * rows, head)

    pulled = jnp.dot(grad_rows, output_full, preferred_element_type=F32)
    dattended = jnp.sum(
        pulled.reshape(rows, experts, head) * output_gate[:, :, None], axis=1
    ).astype(BF16)
    datt_zh = share(dattended, "zh", n_zh).reshape(n_zh * rows, head)
    datt_all = jnp.concatenate([datt_zh, other_core(datt_zh)], axis=0)

    dweights = contract_last(values_x, datt_all)
    delta = jnp.sum(prob_low.astype(F32) * dweights, axis=0).reshape(2, count // 2)
    delta = share(own_first(delta), ("zh", "c"), n_zh * 2)
    row_delta = own_first(jnp.sum(delta, axis=0)).reshape(-1)
    dscores = (attn_prob * (dweights - row_delta[None, :])).astype(BF16)

    key_term = jnp.dot(dscores, queries_all, preferred_element_type=F32) * scale
    value_term = jnp.dot(prob_low, datt_all, preferred_element_type=F32)
    key_value = jnp.concatenate([key_term, value_term], axis=1).astype(BF16)
    key_value = exchange(key_value.reshape(n_x, rows, 2 * head), "x")
    key_value = jnp.sum(key_value.astype(F32), axis=0).astype(BF16)
    grad_keys = key_value[:, :head]
    dvalue = key_value[:, head:]

    attended_term = contract_first(prob_low, values_x)
    query_term = contract_first(dscores, keys_x) * scale
    both = jnp.concatenate([attended_term, query_term], axis=1)
    both = both[: count // 2] + other_core(both[count // 2 :].astype(BF16)).astype(F32)
    both = exchange(both.astype(BF16).reshape(n_zh, rows, 2 * head), "zh")
    both = jnp.sum(both.astype(F32), axis=0).astype(BF16)
    attended = both[:, :head]
    grad_queries = both[:, head:]

    def expand(gate, vec):
        spread = gate[:, :, None] * vec.astype(F32)[:, None, :]
        return spread.reshape(rows, panel_width).astype(BF16)

    layer_output = contract_last(expand(output_gate, attended), output_full).astype(BF16)
    value_grad = expand(value_gate, dvalue)
    grad_tokens = contract_last(value_grad, value_own).astype(BF16)

    term_value = contract_first(tok_block, value_grad)
    term_output = contract_first(grad_rows, expand(output_gate_own, attended))
    theirs = jnp.concatenate([term_value[:, half:], term_output[:, half:]], axis=1)
    mine = jnp.concatenate([term_value[:, :half], term_output[:, :half]], axis=1)
    chip = (mine + other_core(theirs.astype(BF16)).astype(F32)).astype(BF16)
    piece = panel_rows // n_y
    chip = chip.reshape(n_x, n_zh, 2, n_y, piece, panel_width).transpose(0, 3, 1, 2, 4, 5)
    chip = exchange(chip.reshape(n_x * n_y, n_zh * 2 * piece, panel_width), ("x", "y"))
    plane = jnp.sum(chip.astype(F32), axis=0).astype(BF16)
    small = piece // n_zl
    plane = plane.reshape(n_zh, 2, n_zl, small, panel_width).transpose(2, 0, 1, 3, 4)
    plane = exchange(plane.reshape(n_zl * n_zh, 2 * small, panel_width), ("zl", "zh"))
    whole = jnp.sum(plane.astype(F32), axis=0).astype(BF16).reshape(2, small, panel_width)
    keep = lax.dynamic_index_in_dim(whole, ic, 0, keepdims=False)
    give = lax.dynamic_index_in_dim(whole, 1 - ic, 0, keepdims=False)
    whole = own_first(jnp.stack([keep, other_core(give)]))
    whole = share(whole, ("zl", "y"), n_zl * n_y)
    whole = whole.reshape(n_zl, n_y, 2, small, 2, half).transpose(4, 1, 0, 3, 2, 5)
    grads = whole.reshape(2, panel_rows, panel_width).astype(F32)
    return (
        layer_output[None],
        grad_tokens[None],
        grad_queries[None],
        grad_keys[None],
        grads[0],
        grads[1],
    )


def solution(mesh):
    chips = Mesh(mesh.devices.reshape(2, 4, 4, 4, 2), ("zl", "y", "x", "zh", "c"))
    batch, place = ("zl", "y"), ("x", "zh", "c")
    wide = P(batch, place, None)
    panel = P(place, None)
    in_specs = (wide, wide, wide, P(batch, place), wide, wide, wide, wide, panel, panel, wide)
    out_specs = (wide, wide, wide, wide, panel, panel)
    return jax.shard_map(
        body, mesh=chips, in_specs=in_specs, out_specs=out_specs, check_vma=False
    )
```

time: 668 us -> 351 us (0.53)
  waiting for transfers between devices: 553 us -> 106 us
  starting transfers between devices: 0.72 us -> 67.6 us
  blocking collectives: 0 us -> 54.5 us
  other arithmetic: 11.8 us -> 27.6 us
  matrix products: 52 us -> 40.5 us
    all_gather x4 -> x1, waiting for transfers between devices: 207 us -> 0.02 us  [body(): lax.all_gather(output_panels, ('x', 'zh', 'c'), axis=0, tiled=True)]
    reduce_scatter x2 -> x0, waiting for transfers between devices: 176 us -> none  [the longest x1 95.6 us: body(): lax.psum_scatter(key_term.astype(jnp.bfloat16), 'seq', scatter_dimension=...]
    unnamed x9 -> x1, waiting for transfers between devices: 112 us -> 0.68 us
    all_to_all x0 -> x10, waiting for transfers between devices: none -> 97.2 us  [exchange(): return lax.all_to_all(blocks, axes, 0, 0, tiled=True)]
    psum x1 -> x0, waiting for transfers between devices: 58.4 us -> none  [body(): summed = lax.psum(owned, 'dp').astype(jnp.float32)]
    all_to_all x0 -> x1, blocking collectives: none -> 54.5 us  [exchange(): return lax.all_to_all(blocks, axes, 0, 0, tiled=True)]
    all_to_all x0 -> x10, starting transfers between devices: none -> 43.8 us  [exchange(): return lax.all_to_all(blocks, axes, 0, 0, tiled=True)]
    ppermute x0 -> x8, starting transfers between devices: none -> 23.7 us  [other_core(): return lax.ppermute(value, 'c', [(0, 1), (1, 0)])]
  transfers between devices with their start and end apart: 8 -> 19, of which waited for: 8 -> 12; matrix products, arithmetic and copies ran while one was open for 9% -> 17% of each run, Pallas kernels for 0% -> 0%
where the time goes in v1:
time: 351 us; the launch traced here: 349 us
  waiting for transfers between devices  106 us (30%)
  starting transfers between devices  67.6 us (19%)
  blocking collectives  54.5 us (16%)
  matrix products  40.5 us (12%)
  local copies, waits for them, and re-layouts  38.4 us (11%)
  other arithmetic  27.6 us (8%)
  between operations  14.7 us (4%)
    all_to_all x10, waiting for transfers between devices, exchange(): return lax.all_to_all(blocks, axes, 0, 0, tiled=True)  97.2 us
    all_to_all x1, blocking collectives, exchange(): return lax.all_to_all(blocks, axes, 0, 0, tiled=True)  54.5 us
    all_to_all x10, starting transfers between devices, exchange(): return lax.all_to_all(blocks, axes, 0, 0, tiled=True)  43.8 us
    ppermute x8, starting transfers between devices, other_core(): return lax.ppermute(value, 'c', [(0, 1), (1, 0)])  23.7 us
    dot_general x4, matrix products, contract_last(): lax.dot_general(left, right, (((1,), (1,)), ((), ())), preferred_element_...  22.4 us
    dot_general x4, matrix products, contract_first(): lax.dot_general(left, right, (((0,), (0,)), ((), ())), preferred_element_...  7.97 us
    ppermute x8, waiting for transfers between devices, other_core(): return lax.ppermute(value, 'c', [(0, 1), (1, 0)])  7.76 us
    convert_element_type x1, other arithmetic, body(): dscores = (attn_prob * (dweights - row_delta[None, :])).astype(BF16)  7.08 us
  transfers between devices with their start and end apart: 19, of which 12 were waited for; matrix products, arithmetic and copies ran while one was open for 17% of the time, Pallas kernels for 0%

profile of v1, /device:TPU:1, one launch (start us, length us, event | category | flops | bytes accessed | tf_op | source)
XLA Modules:
  0.0 349.0 jit_solution(17144868760256053533)
XLA Ops:
  15.7 6.4 %all-to-all-start = ((bf16[4,272,384]{2,1,0:T(8,128)(2,1)}), bf16[4,272,384]{2,1,0:T(8,128)(2,1)S(1)}, u32[]{:S(2)}, u32[]{:S(2)}) async-start(bf16[4,272,384]{2,1,0:T(8,128)(2,1)} %broadcast_in_dim.32), calls=%async_computation | async-start | bytes 1671168 | tf_op jit(solution)/shard_map/all_to_all | solution.py:24
  23.6 22.1 %all-to-all-done = bf16[4,272,384]{2,1,0:T(8,128)(2,1)S(1)} async-done(((bf16[4,272,384]{2,1,0:T(8,128)(2,1)}), bf16[4,272,384]{2,1,0:T(8,128)(2,1)S(1)}, u32[]{:S(2)}, u32[]{:S(2)}) %all-to-all-start) | async-done | bytes 835616 | tf_op jit(solution)/shard_map/all_to_all | solution.py:24
  47.4 4.5 %all-to-all-start.1 = ((bf16[4,1152,256]{2,1,0:T(8,128)(2,1)}), bf16[4,1152,256]{2,1,0:T(8,128)(2,1)}, u32[]{:S(2)}, u32[]{:S(2)}) async-start(bf16[4,1152,256]{2,1,0:T(8,128)(2,1)} %broadcast_in_dim.33), calls=%async_computation.1 | async-start | bytes 4718592 | tf_op jit(solution)/shard_map/all_to_all | solution.py:24
  57.0 28.7 %all-to-all-done.1 = bf16[4,1152,256]{2,1,0:T(8,128)(2,1)} async-done(((bf16[4,1152,256]{2,1,0:T(8,128)(2,1)}), bf16[4,1152,256]{2,1,0:T(8,128)(2,1)}, u32[]{:S(2)}, u32[]{:S(2)}) %all-to-all-start.1) | async-done | bytes 2359328 | tf_op jit(solution)/shard_map/all_to_all | solution.py:24
  88.7 4.9 %collective-permute-start.3 = (bf16[4096,256]{1,0:T(8,128)(2,1)}, bf16[4096,256]{1,0:T(8,128)(2,1)}, u32[]{:S(2)}, u32[]{:S(2)}) collective-permute-start(bf16[4096,256]{1,0:T(8,128)(2,1)} %bitcast.16), channel_id=1, source_target_pairs={{0,1},{1,0},{2,3},{3,2},{4,5},{5,4},{6,7},{7,6},{8,9},{9,8},{10,11... | collective-permute-start | bytes 6291464 | tf_op jit(solution)/shard_map/ppermute | solution.py:32
  94.6 4.3 %fusion.40 = (f32[2048]{0:T(1024)S(1)}, f32[1024,2048]{1,0:T(8,128)}) fusion(bf16[1024,128]{1,0:T(8,128)(2,1)S(1)} %bitcast.151, bf16[1024,128]{1,0:T(8,128)(2,1)S(1)} %collective-permute-done.2, bf16[1024,128]{1,0:T(8,128)(2,1)S(1)} %bitcast.163, s32[2048]{0:T(1024)S(1)} %sub.55, s32[2048]{0:T(1024)S(1)} %bitcast.180, s32[1024]{0:T(1024)S(1)} %bitcast.183), kind=kOutput, calls=%fused_computation.114 | convolution fusion | flops 550500352 | bytes 9203712 | tf_op jit(solution)/shard_map/dot_general | solution.py:16
  99.0 4.6 %exponential_reduce_fusion = f32[2048]{0:T(1024)S(1)} fusion(f32[1024,2048]{1,0:T(8,128)} %get-tuple-element.71, f32[2048]{0:T(1024)S(1)} %broadcast_maximum_fusion), kind=kLoop, calls=%fused_computation.5 | loop fusion | flops 4192256 | bytes 8404992 | tf_op jit(solution)/shard_map/reduce_sum | solution.py:117
  104.5 6.0 %all-to-all-start.2 = ((f32[8,2,2,1024]{3,2,1,0:T(2,128)}), f32[8,2,2,1024]{3,2,1,0:T(2,128)S(1)}, u32[]{:S(2)}, u32[]{:S(2)}) async-start(f32[8,2,2,1024]{3,2,1,0:T(2,128)} %broadcast_in_dim.35), calls=%async_computation.2 | async-start | bytes 262144 | tf_op jit(solution)/shard_map/all_to_all | solution.py:24
  110.6 8.0 %all-to-all-done.2 = f32[8,2,2,1024]{3,2,1,0:T(2,128)S(1)} async-done(((f32[8,2,2,1024]{3,2,1,0:T(2,128)}), f32[8,2,2,1024]{3,2,1,0:T(2,128)S(1)}, u32[]{:S(2)}, u32[]{:S(2)}) %all-to-all-start.2) | async-done | bytes 131104 | tf_op jit(solution)/shard_map/all_to_all | solution.py:24
  119.0 6.4 %copy.78 = bf16[512,4096]{1,0:T(8,128)(2,1)} copy(bf16[512,4096]{0,1:T(8,128)(2,1)} %bitcast.139) | data formatting | bytes 8388608 | tf_op jit(solution)/shard_map/dot_general | solution.py:133
  137.2 4.6 %all-to-all-done.4 = bf16[4,256,128]{2,1,0:T(8,128)(2,1)S(1)} async-done(((bf16[4,256,128]{2,1,0:T(8,128)(2,1)}), bf16[4,256,128]{2,1,0:T(8,128)(2,1)S(1)}, u32[]{:S(2)}, u32[]{:S(2)}) %all-to-all-start.4) | async-done | bytes 262176 | tf_op jit(solution)/shard_map/all_to_all | solution.py:24
  149.9 6.6 %all-to-all-done.3 = bf16[4,256,128]{2,1,0:T(8,128)(2,1)S(1)} async-done(((bf16[4,256,128]{2,1,0:T(8,128)(2,1)}), bf16[4,256,128]{2,1,0:T(8,128)(2,1)S(1)}, u32[]{:S(2)}, u32[]{:S(2)}) %all-to-all-start.3) | async-done | bytes 262176 | tf_op jit(solution)/shard_map/all_to_all | solution.py:24
  156.5 8.3 %multiply_reduce_fusion = (f32[2048]{0:T(1024)S(1)}, bf16[1024,2048]{1,0:T(8,128)(2,1)}, f32[1024,2048]{1,0:T(8,128)}) fusion(f32[1024,2048]{1,0:T(8,128)} %get-tuple-element.71, f32[2048]{0:T(1024)S(1)} %bitcast.170, bf16[1024,128]{1,0:T(8,128)(2,1)S(1)} %bitcast.143, bf16[1024,128]{1,0:T(8,128)(2,1)S(1)} %collective-permute-done.4, ...), kind=kOutput, calls=%fused_computation.3 | convolution fusion | flops 548403200 | bytes 21774336 | tf_op jit(solution)/shard_map/dot_general | solution.py:16
  177.4 7.1 %multiply_convert_fusion = bf16[1024,2048]{1,0:T(8,128)(2,1)S(1)} fusion(f32[1024,2048]{1,0:T(8,128)} %get-tuple-element.72, f32[1024,2048]{1,0:T(8,128)} %get-tuple-element.71, f32[2048]{0:T(1024)S(1)} %bitcast.177, f32[2048]{0:T(1024)S(1)} %bitcast.171), kind=kLoop, calls=%fused_computation.2 | loop fusion | flops 8388608 | bytes 20987904 | tf_op jit(solution)/shard_map/convert_element_type | solution.py:144
  189.4 4.1 %all-to-all-start.7 = ((bf16[4,256,256]{2,1,0:T(8,128)(2,1)}), bf16[4,256,256]{2,1,0:T(8,128)(2,1)}, u32[]{:S(2)}, u32[]{:S(2)}) async-start(bf16[4,256,256]{2,1,0:T(8,128)(2,1)} %pad_maximum_fusion.7), calls=%async_computation.7 | async-start | bytes 1048576 | tf_op jit(solution)/shard_map/all_to_all | solution.py:24
  193.6 9.7 %all-to-all-done.7 = bf16[4,256,256]{2,1,0:T(8,128)(2,1)} async-done(((bf16[4,256,256]{2,1,0:T(8,128)(2,1)}), bf16[4,256,256]{2,1,0:T(8,128)(2,1)}, u32[]{:S(2)}, u32[]{:S(2)}) %all-to-all-start.7) | async-done | bytes 524320 | tf_op jit(solution)/shard_map/all_to_all | solution.py:24
  215.6 7.3 %all-to-all-done.6 = bf16[4,256,256]{1,2,0:T(8,128)(2,1)S(1)} async-done(((bf16[4,256,256]{1,2,0:T(8,128)(2,1)}), bf16[4,256,256]{1,2,0:T(8,128)(2,1)S(1)}, u32[]{:S(2)}, u32[]{:S(2)}) %all-to-all-start.6) | async-done | bytes 524320 | tf_op jit(solution)/shard_map/all_to_all | solution.py:24
  231.6 6.3 %collective-permute-done.6 = bf16[4096,512]{0,1:T(8,128)(2,1)S(1)} collective-permute-done((bf16[4096,512]{0,1:T(8,128)(2,1)S(1)}, bf16[4096,512]{0,1:T(8,128)(2,1)S(1)}, u32[]{:S(2)}, u32[]{:S(2)}) %collective-permute-start.6) | collective-permute-done | bytes 4194336 | tf_op jit(solution)/shard_map/ppermute | solution.py:32
  240.9 6.5 %copy.86 = bf16[4096,512]{1,0:T(8,128)(2,1)} copy(bf16[4096,512]{0,1:T(8,128)(2,1)} %fusion) | data formatting | bytes 8388608 | tf_op jit(solution)/shard_map/convert_element_type | solution.py:175
  250.0 54.5 %all_to_all.55 = bf16[16,256,512]{2,1,0:T(8,128)(2,1)} all-to-all(bf16[16,256,512]{2,1,0:T(8,128)(2,1)S(1)} %bitcast.141), channel_id=1, replica_groups=mesh['zl'=2,'y'=4,'x'=4,'zh'=4,'c'=2] {'x','y'}, dimensions={0} | all-to-all | bytes 8388608 | tf_op jit(solution)/shard_map/all_to_all | solution.py:24
  311.6 7.7 %all-to-all-done.9 = bf16[8,32,512]{2,1,0:T(8,128)(2,1)S(1)} async-done(((bf16[8,32,512]{2,1,0:T(8,128)(2,1)}), bf16[8,32,512]{2,1,0:T(8,128)(2,1)S(1)}, u32[]{:S(2)}, u32[]{:S(2)}) %all-to-all-start.9) | async-done | bytes 262176 | tf_op jit(solution)/shard_map/all_to_all | solution.py:24
  323.9 4.7 %all-to-all-start.10 = ((bf16[8,2,16,512]{3,2,1,0:T(8,128)(2,1)}), bf16[8,2,16,512]{3,2,1,0:T(8,128)(2,1)S(1)}, u32[]{:S(2)}, u32[]{:S(2)}) async-start(bf16[8,2,16,512]{3,2,1,0:T(8,128)(2,1)} %broadcast_in_dim.43), calls=%async_computation.10 | async-start | bytes 524288 | tf_op jit(solution)/shard_map/all_to_all | solution.py:24
  328.7 4.9 %fusion.3 = bf16[1,256,4096]{2,1,0:T(8,128)(2,1)} fusion(bf16[256,512]{0,1:T(8,128)(2,1)S(1)} %bitcast.158, bf16[4096,256]{1,0:T(8,128)(2,1)} %collective-permute-done.3, bf16[4096,256]{1,0:T(8,128)(2,1)} %bitcast.16), kind=kOutput, calls=%fused_computation.13 | convolution fusion | flops 1083179008 | bytes 6553600 | tf_op jit(solution)/shard_map/dot_general | solution.py:16
  334.4 5.0 %fusion.2 = bf16[1,256,4096]{2,1,0:T(8,128)(2,1)} fusion(bf16[256,512]{0,1:T(8,128)(2,1)S(1)} %bitcast.153, bf16[4096,512]{1,0:T(8,128)(2,1)} %all-gather.2.cloned.1.call-done), kind=kOutput, calls=%fused_computation.12 | convolution fusion | flops 1074790400 | bytes 6553600 | tf_op jit(solution)/shard_map/dot_general | solution.py:16
  (171 shorter events, 101.1 us)
Async XLA Ops:
  7.2 126.5 %copy-start = (bf16[1,256,4096]{2,1,0:T(8,128)(2,1)S(1)}, bf16[1,256,4096]{2,1,0:T(8,128)(2,1)}, u32[]{:S(2)}) copy-start(bf16[1,256,4096]{2,1,0:T(8,128)(2,1)} %param.15) | copy-start | bytes 6291460
  7.2 16.4 %copy-start.13 = (bf16[1,256,128]{2,1,0:T(8,128)(2,1)S(1)}, bf16[1,256,128]{2,1,0:T(8,128)(2,1)}, u32[]{:S(2)}) copy-start(bf16[1,256,128]{2,1,0:T(8,128)(2,1)} %param.17) | copy-start | bytes 196612
  7.2 111.8 %all-gather.2.cloned.1.call-start = ((), (), s32[]{:S(2)}) async-start(), calls=%async_computation.11 | async-start | bytes 4325376 | tf_op jit(solution)/shard_map/all_gather | solution.py:72
  8.8 4.9 %collective-permute-start = (bf16[128,256]{1,0:T(8,128)(2,1)S(1)}, bf16[128,256]{1,0:T(8,128)(2,1)S(1)}, u32[]{:S(2)}, u32[]{:S(2)}) collective-permute-start(bf16[128,256]{1,0:T(8,128)(2,1)S(1)} %get-tuple-element.65), channel_id=1, source_target_pairs={{0,1},{1,0},{2,3},{3,2},{4,5},{5,4},{6,7},{7,6},{8,9},{9,8},{10,11... | collective-permute-start | bytes 196616 | tf_op jit(solution)/shard_map/ppermute | solution.py:32
  15.7 30.1 %all-to-all-start = ((bf16[4,272,384]{2,1,0:T(8,128)(2,1)}), bf16[4,272,384]{2,1,0:T(8,128)(2,1)S(1)}, u32[]{:S(2)}, u32[]{:S(2)}) async-start(bf16[4,272,384]{2,1,0:T(8,128)(2,1)} %broadcast_in_dim.32), calls=%async_computation | async-start | bytes 1671168 | tf_op jit(solution)/shard_map/all_to_all | solution.py:24
  47.4 38.2 %all-to-all-start.1 = ((bf16[4,1152,256]{2,1,0:T(8,128)(2,1)}), bf16[4,1152,256]{2,1,0:T(8,128)(2,1)}, u32[]{:S(2)}, u32[]{:S(2)}) async-start(bf16[4,1152,256]{2,1,0:T(8,128)(2,1)} %broadcast_in_dim.33), calls=%async_computation.1 | async-start | bytes 4718592 | tf_op jit(solution)/shard_map/all_to_all | solution.py:24
  52.1 4.8 %collective-permute-start.1 = (bf16[4,2,256]{2,1,0:T(2,128)(2,1)S(1)}, bf16[4,2,256]{2,1,0:T(2,128)(2,1)S(1)}, u32[]{:S(2)}, u32[]{:S(2)}) collective-permute-start(bf16[4,2,256]{2,1,0:T(2,128)(2,1)S(1)} %get-tuple-element.55), channel_id=1, source_target_pairs={{0,1},{1,0},{2,3},{3,2},{4,5},{5,4},{6,7},{7,6},{8,9},{9,8},{10,11... | collective-permute-start | bytes 12296 | tf_op jit(solution)/shard_map/ppermute | solution.py:32
  56.3 42.7 %copy-start.11 = (bf16[4,256,128]{2,1,0:T(8,128)(2,1)}, bf16[4,256,128]{2,1,0:T(8,128)(2,1)S(1)}, u32[]{:S(2)}) copy-start(bf16[4,256,128]{2,1,0:T(8,128)(2,1)S(1)} %slice.154) | copy-start | bytes 786436
  56.3 38.3 %collective-permute-start.2 = (bf16[1024,128]{1,0:T(8,128)(2,1)S(1)}, bf16[1024,128]{1,0:T(8,128)(2,1)S(1)}, u32[]{:S(2)}, u32[]{:S(2)}) collective-permute-start(bf16[1024,128]{1,0:T(8,128)(2,1)S(1)} %bitcast.162), channel_id=1, source_target_pairs={{0,1},{1,0},{2,3},{3,2},{4,5},{5,4},{6,7},{7,6},{8,9},{9,8},{10,11... | collective-permute-start | bytes 786440 | tf_op jit(solution)/shard_map/ppermute | solution.py:32
  88.7 44.9 %collective-permute-start.3 = (bf16[4096,256]{1,0:T(8,128)(2,1)}, bf16[4096,256]{1,0:T(8,128)(2,1)}, u32[]{:S(2)}, u32[]{:S(2)}) collective-permute-start(bf16[4096,256]{1,0:T(8,128)(2,1)} %bitcast.16), channel_id=1, source_target_pairs={{0,1},{1,0},{2,3},{3,2},{4,5},{5,4},{6,7},{7,6},{8,9},{9,8},{10,11... | collective-permute-start | bytes 6291464 | tf_op jit(solution)/shard_map/ppermute | solution.py:32
  99.0 11.6 %copy-start.14 = (f32[1,256,4]{1,2,0:T(4,128)S(1)}, f32[1,256,4]{1,2,0:T(4,128)}, u32[]{:S(2)}) copy-start(f32[1,256,4]{1,2,0:T(4,128)} %param.21) | copy-start | bytes 12292
  104.5 14.0 %all-to-all-start.2 = ((f32[8,2,2,1024]{3,2,1,0:T(2,128)}), f32[8,2,2,1024]{3,2,1,0:T(2,128)S(1)}, u32[]{:S(2)}, u32[]{:S(2)}) async-start(f32[8,2,2,1024]{3,2,1,0:T(2,128)} %broadcast_in_dim.35), calls=%async_computation.2 | async-start | bytes 262144 | tf_op jit(solution)/shard_map/all_to_all | solution.py:24
  130.2 11.5 %all-to-all-start.4 = ((bf16[4,256,128]{2,1,0:T(8,128)(2,1)}), bf16[4,256,128]{2,1,0:T(8,128)(2,1)S(1)}, u32[]{:S(2)}, u32[]{:S(2)}) async-start(bf16[4,256,128]{2,1,0:T(8,128)(2,1)} %broadcast_in_dim.37), calls=%async_computation.4 | async-start | bytes 524288 | tf_op jit(solution)/shard_map/all_to_all | solution.py:24
  141.7 23.1 %copy-start.5 = (bf16[4,256,128]{2,1,0:T(8,128)(2,1)}, bf16[4,256,128]{2,1,0:T(8,128)(2,1)S(1)}, u32[]{:S(2)}) copy-start(bf16[4,256,128]{2,1,0:T(8,128)(2,1)S(1)} %all-to-all-done.4) | copy-start | bytes 786436
  141.7 14.7 %collective-permute-start.4 = (bf16[1024,128]{1,0:T(8,128)(2,1)S(1)}, bf16[1024,128]{1,0:T(8,128)(2,1)S(1)}, u32[]{:S(2)}, u32[]{:S(2)}) collective-permute-start(bf16[1024,128]{1,0:T(8,128)(2,1)S(1)} %bitcast.148), channel_id=1, source_target_pairs={{0,1},{1,0},{2,3},{3,2},{4,5},{5,4},{6,7},{7,6},{8,9},{9,8},{10,11... | collective-permute-start | bytes 786440 | tf_op jit(solution)/shard_map/ppermute | solution.py:32
  146.2 10.2 %all-to-all-start.3 = ((bf16[4,256,128]{2,1,0:T(8,128)(2,1)}), bf16[4,256,128]{2,1,0:T(8,128)(2,1)S(1)}, u32[]{:S(2)}, u32[]{:S(2)}) async-start(bf16[4,256,128]{2,1,0:T(8,128)(2,1)} %broadcast_in_dim.36), calls=%async_computation.3 | async-start | bytes 524288 | tf_op jit(solution)/shard_map/all_to_all | solution.py:24
  165.7 11.4 %all-to-all-start.5 = ((f32[8,2,1024]{2,1,0:T(2,128)}), f32[8,2,1024]{2,1,0:T(2,128)S(1)}, u32[]{:S(2)}, u32[]{:S(2)}) async-start(f32[8,2,1024]{2,1,0:T(2,128)} %broadcast_in_dim.38), calls=%async_computation.5 | async-start | bytes 131072 | tf_op jit(solution)/shard_map/all_to_all | solution.py:24
  186.3 18.1 %collective-permute-start.5 = (bf16[1024,256]{0,1:T(8,128)(2,1)}, bf16[1024,256]{0,1:T(8,128)(2,1)}, u32[]{:S(2)}, u32[]{:S(2)}) collective-permute-start(bf16[1024,256]{0,1:T(8,128)(2,1)} %fusion.20), channel_id=1, source_target_pairs={{0,1},{1,0},{2,3},{3,2},{4,5},{5,4},{6,7},{7,6},{8,9},{9,8},{10,11... | collective-permute-start | bytes 1572872 | tf_op jit(solution)/shard_map/ppermute | solution.py:32
  189.4 13.9 %all-to-all-start.7 = ((bf16[4,256,256]{2,1,0:T(8,128)(2,1)}), bf16[4,256,256]{2,1,0:T(8,128)(2,1)}, u32[]{:S(2)}, u32[]{:S(2)}) async-start(bf16[4,256,256]{2,1,0:T(8,128)(2,1)} %pad_maximum_fusion.7), calls=%async_computation.7 | async-start | bytes 1048576 | tf_op jit(solution)/shard_map/all_to_all | solution.py:24
  206.6 16.4 %all-to-all-start.6 = ((bf16[4,256,256]{1,2,0:T(8,128)(2,1)}), bf16[4,256,256]{1,2,0:T(8,128)(2,1)S(1)}, u32[]{:S(2)}, u32[]{:S(2)}) async-start(bf16[4,256,256]{1,2,0:T(8,128)(2,1)} %bitcast.136), calls=%async_computation.6 | async-start | bytes 1048576 | tf_op jit(solution)/shard_map/all_to_all | solution.py:24
  227.3 10.7 %collective-permute-start.6 = (bf16[4096,512]{0,1:T(8,128)(2,1)S(1)}, bf16[4096,512]{0,1:T(8,128)(2,1)S(1)}, u32[]{:S(2)}, u32[]{:S(2)}) collective-permute-start(bf16[4096,512]{0,1:T(8,128)(2,1)S(1)} %pad_maximum_fusion.1), channel_id=1, source_target_pairs={{0,1},{1,0},{2,3},{3,2},{4,5},{5,4},{6,7},{7,6},{8,9},{9,8},{10,11... | collective-permute-start | bytes 12582920 | tf_op jit(solution)/shard_map/ppermute | solution.py:32
  308.1 11.2 %all-to-all-start.9 = ((bf16[8,32,512]{2,1,0:T(8,128)(2,1)}), bf16[8,32,512]{2,1,0:T(8,128)(2,1)S(1)}, u32[]{:S(2)}, u32[]{:S(2)}) async-start(bf16[8,32,512]{2,1,0:T(8,128)(2,1)} %bitcast.48), calls=%async_computation.9 | async-start | bytes 524288 | tf_op jit(solution)/shard_map/all_to_all | solution.py:24
  319.4 3.8 %collective-permute-start.7 = (bf16[16,512]{1,0:T(8,128)(2,1)S(1)}, bf16[16,512]{1,0:T(8,128)(2,1)S(1)}, u32[]{:S(2)}, u32[]{:S(2)}) collective-permute-start(bf16[16,512]{1,0:T(8,128)(2,1)S(1)} %get-tuple-element.69), channel_id=1, source_target_pairs={{0,1},{1,0},{2,3},{3,2},{4,5},{5,4},{6,7},{7,6},{8,9},{9,8},{10,11... | collective-permute-start | bytes 49160 | tf_op jit(solution)/shard_map/ppermute | solution.py:32
  323.9 15.4 %all-to-all-start.10 = ((bf16[8,2,16,512]{3,2,1,0:T(8,128)(2,1)}), bf16[8,2,16,512]{3,2,1,0:T(8,128)(2,1)S(1)}, u32[]{:S(2)}, u32[]{:S(2)}) async-start(bf16[8,2,16,512]{3,2,1,0:T(8,128)(2,1)} %broadcast_in_dim.43), calls=%async_computation.10 | async-start | bytes 524288 | tf_op jit(solution)/shard_map/all_to_all | solution.py:24
  (14 other events, 72.6 us)
Sparse Core Ops, SparseCore 0:
  10.6 72.6 all-gather.1
